TPU v7x, 32 devices: a whole 2x2x4 slice. The times are simulated.
32 devices in a mesh: groups: 2 (over y), dp: 4 (over z), rep: 4 (over x, core).
Axes of the slice: x: 2, y: 2, z: 4, core: 2. Of those that a mesh axis runs over, the one named last changes fastest.
Arguments:
- latent_store: bfloat16 [8, 48, 576, 128], P(('groups', 'dp'), 'rep'), parts along dimension 0, may hold values from -6 to 6
- page_rank: int32 [8, 48], P('groups', 'rep'), parts along dimension 0, may hold values from 0 to 3, as said below
- page_index: int32 [8, 48], P('groups', 'rep'), parts along dimension 0, may hold values from 0 to 11, as said below
- lengths: int32 [8, 1], P('groups'), parts along dimension 0, may hold values from 1536 to 6144, as said below
- queries: bfloat16 [16, 36864], P(('groups', 'dp')), parts along dimension 0, may hold values from -250 to 250
- new_latent: bfloat16 [16, 576], P(('groups', 'dp')), parts along dimension 0, may hold values from -4 to 4
- up_value: bfloat16 [64, 512, 128], P('dp'), may hold values from -0.25 to 0.25
- out_proj: bfloat16 [8192, 7168], P('dp', 'rep'), may hold values from -0.0625 to 0.0625
- residual: bfloat16 [16, 7168], P(('groups', 'dp'), 'rep'), parts along dimension 0, may hold values from -11 to 11
- norm_gain: float32 [7168], P('rep'), may hold values from 0.1 to 1.9
- w_gate: bfloat16 [7168, 12288], P('rep', 'dp'), may hold values from -0.0625 to 0.0625
- w_up: bfloat16 [7168, 12288], P('rep', 'dp'), may hold values from -0.0625 to 0.0625
- w_down: bfloat16 [12288, 7168], P('dp', 'rep'), may hold values from -0.0546875 to 0.0546875
Outputs:
- layer_out: bfloat16 [16, 7168], P(('groups', 'dp'), 'rep'), parts along dimension 0
There are 2 independent parts, one for each index of `groups`. A program takes and returns all parts, laid end to end along the dimension named above; an argument that names none is the same for every part. Nothing has to cross between parts.
Inputs may be any that keep to these rules, and one draw needn't show every extreme that they name: page_rank[d, q] is the storage rank holding slot q of rank d, on its device with rep index q // 12; one storage device holds at most 3 slot of one rank, and some holds exactly 3. page_index[d, q] is the slot's page among the 12 pages of its storage device; over all ranks every page of every storage device is named by exactly one slot. `lengths`: some request has exactly 6144 tokens.
All inputs are finite; a program needn't handle non-finite values.
Results may differ from a plain program's by a relative error of at most 0.015.
Values may be sent and summed in bfloat16 or wider, within the bound.
No kernel may reach another device: no remote copies, remote signals or barrier semaphores. Data moves between devices by JAX's collectives and lax.ppermute only.
A program may use at most 128 MiB of HBM per device.

v0:
```python
import math
import jax
import jax.numpy as jnp
from jax import lax
from jax.sharding import PartitionSpec as P

D = 7168
CKV = 512
PAGE = 128
PAGES = 48
score_scale = 1.0 / math.sqrt(192.0)
epsilon = 1e-06
mask_value = -1e30


def merged_2(array, axis, join):
    gathered = jax.tree.map(
        lambda a, kind: lax.all_gather(a.astype(kind), axis),
        array,
        jax.tree.map(lambda a: jnp.bfloat16 if a.dtype == jnp.float32 else a.dtype, array),
    )

    def take(source):
        return jax.tree.map(
            lambda a, own: lax.dynamic_index_in_dim(a, source, 0, False).astype(own.dtype),
            gathered,
            array,
        )

    return lax.fori_loop(
        1, lax.axis_size(axis), lambda source, state: join(state, take(source)), take(0)
    )


def page_partials(page_keys, page_queries, key_counts):
    scores = (
        jnp.einsum("pshl,plt->psht", page_queries, page_keys, preferred_element_type=jnp.float32)
        * score_scale
    )
    places = lax.broadcasted_iota(jnp.int32, scores.shape, 3)
    visible = places < key_counts[:, None, None, None]
    scores = jnp.where(visible, scores, mask_value)
    row_peak = jnp.max(scores, axis=3)
    weights = jnp.where(visible, jnp.exp(scores - row_peak[..., None]), 0.0)
    row_total = jnp.sum(weights, axis=3)
    partial_value = jnp.einsum(
        "psht,pct->pshc",
        weights.astype(jnp.bfloat16),
        page_keys[:, :CKV, :],
        preferred_element_type=jnp.float32,
    )
    return (partial_value, row_peak, row_total)


def join_pages(partial_value, row_peak, row_total, slot_request, requests):
    owner_mask = slot_request[None, :] == jnp.arange(requests, dtype=jnp.int32)[:, None]
    spread = owner_mask[:, :, None, None]
    best_peak = jnp.max(jnp.where(spread, row_peak[None], mask_value), axis=1)
    factor = jnp.where(spread, jnp.exp(row_peak[None] - best_peak[:, None]), 0.0)
    joined = jnp.einsum("jpsh,pshc->jshc", factor, partial_value, precision=lax.Precision.HIGHEST)
    summed = jnp.sum(factor * row_total[None], axis=1)
    return (joined, best_peak, summed)


def combine(former, latter):
    former_sum, former_peak, former_total = former
    latter_sum, latter_peak, latter_total = latter
    highest = jnp.maximum(former_peak, latter_peak)
    former_scale = jnp.exp(former_peak - highest)
    latter_scale = jnp.exp(latter_peak - highest)
    merged_sum = former_sum * former_scale[..., None] + latter_sum * latter_scale[..., None]
    return (merged_sum, highest, former_total * former_scale + latter_total * latter_scale)


def fresh_partial(query_rows, fresh_rows, active):
    scores = (
        jnp.einsum("jshl,jul->jshu", query_rows, fresh_rows, preferred_element_type=jnp.float32)
        * score_scale
    )
    step_query = lax.broadcasted_iota(jnp.int32, scores.shape, 1)
    step_key = lax.broadcasted_iota(jnp.int32, scores.shape, 3)
    visible = (step_key <= step_query) & active
    scores = jnp.where(visible, scores, mask_value)
    row_peak = jnp.max(scores, axis=3)
    weights = jnp.where(visible, jnp.exp(scores - row_peak[..., None]), 0.0)
    row_total = jnp.sum(weights, axis=3)
    partial_value = jnp.einsum(
        "jshu,juc->jshc",
        weights.astype(jnp.bfloat16),
        fresh_rows[:, :, :CKV],
        preferred_element_type=jnp.float32,
    )
    return (partial_value, row_peak, row_total)


def on_device(
    latent_store,
    page_rank,
    page_index,
    lengths,
    queries,
    new_latent,
    up_value,
    out_proj,
    residual,
    norm_gain,
    w_gate,
    w_up,
    w_down,
):
    my_rank = lax.axis_index("dp")
    my_column = lax.axis_index("rep")
    rank_count, slot_count = page_rank.shape
    capacity = (slot_count + rank_count - 1) // rank_count
    requests = lengths.shape[1]
    rows_here = residual.shape[0]
    steps_count = rows_here // requests
    latent_width = new_latent.shape[1]
    head_count = queries.shape[1] // latent_width
    query_rows = queries.reshape(requests, steps_count, head_count, latent_width)
    fresh_rows = new_latent.reshape(requests, steps_count, latent_width)
    slot_order = jnp.arange(slot_count, dtype=jnp.int32)
    request_ids = jnp.arange(requests, dtype=jnp.int32)
    cap_ids = jnp.arange(capacity, dtype=jnp.int32)
    global_slot = my_column * slot_count + slot_order
    slot_request = global_slot // PAGES
    slot_page = global_slot % PAGES
    own_lengths = lax.dynamic_index_in_dim(lengths, my_rank, 0, keepdims=False)
    slot_length = jnp.sum(
        jnp.where(slot_request[:, None] == request_ids[None, :], own_lengths[None, :], 0), axis=1
    )
    key_counts = jnp.clip(slot_length - slot_page * PAGE, 0, PAGE)
    my_sources = lax.dynamic_index_in_dim(page_rank, my_rank, 0, keepdims=False)
    earlier = (my_sources[None, :] == my_sources[:, None]) & (
        slot_order[None, :] < slot_order[:, None]
    )
    arrival_rank = jnp.sum(earlier.astype(jnp.int32), axis=1)
    arrival_slot = my_sources * capacity + arrival_rank
    held_here = page_rank == my_rank
    held_order = jnp.cumsum(held_here.astype(jnp.int32), axis=1) - 1
    selector = held_here[:, None, :] & (held_order[:, None, :] == cap_ids[None, :, None])
    sent_valid = jnp.any(selector, axis=2).reshape(-1)
    sent_page = jnp.sum(jnp.where(selector, page_index[:, None, :], 0), axis=2).reshape(-1)
    stored = latent_store[0]
    outgoing = jnp.take(stored, sent_page, axis=0)
    outgoing = jnp.where(sent_valid[:, None, None], outgoing, jnp.zeros_like(outgoing))
    arrived = lax.all_to_all(outgoing, "dp", split_axis=0, concat_axis=0, tiled=True)
    restored = jnp.take(arrived, arrival_slot, axis=0)
    page_queries = jnp.take(query_rows, slot_request, axis=0)
    partial_value, row_peak, row_total = page_partials(restored, page_queries, key_counts)
    joined = join_pages(partial_value, row_peak, row_total, slot_request, requests)
    local_part = combine(joined, fresh_partial(query_rows, fresh_rows, my_column == 0))
    merged = merged_2(local_part, "rep", combine)
    attention = (
        (merged[0] / merged[2][..., None]).astype(jnp.bfloat16).reshape(rows_here, head_count, CKV)
    )
    headed = lax.all_to_all(attention, "dp", split_axis=1, concat_axis=0, tiled=True)
    values = jnp.einsum("rhc,hcv->rhv", headed, up_value, preferred_element_type=jnp.float32)
    values = values.astype(jnp.bfloat16).reshape(headed.shape[0], -1)
    picked = values
    attn_out = lax.psum_scatter(
        jnp.dot(picked, out_proj, preferred_element_type=jnp.float32).astype(jnp.bfloat16),
        "dp",
        scatter_dimension=0,
        tiled=True,
    ).astype(jnp.float32)
    mixed_rows = residual.astype(jnp.float32) + attn_out
    squares = lax.psum(jnp.sum(mixed_rows * mixed_rows, axis=1), "rep")
    normed = (mixed_rows * lax.rsqrt(squares / D + epsilon)[:, None] * norm_gain).astype(
        jnp.bfloat16
    )
    piece = lax.all_gather(normed, "dp", axis=0, tiled=True)
    gate_part = jnp.dot(piece, w_gate, preferred_element_type=jnp.float32)
    up_part = jnp.dot(piece, w_up, preferred_element_type=jnp.float32)
    partial_rows = jnp.concatenate([gate_part, up_part], axis=1)
    gate_up = lax.psum(partial_rows.astype(jnp.bfloat16), "rep").astype(jnp.float32)
    hidden_width = w_gate.shape[1]
    hidden = (jax.nn.silu(gate_up[:, :hidden_width]) * gate_up[:, hidden_width:]).astype(
        jnp.bfloat16
    )
    picked = hidden
    mlp_out = lax.psum_scatter(
        jnp.dot(picked, w_down, preferred_element_type=jnp.float32).astype(jnp.bfloat16),
        "dp",
        scatter_dimension=0,
        tiled=True,
    ).astype(jnp.float32)
    return (mixed_rows + mlp_out).astype(jnp.bfloat16)


def solution(mesh):
    in_specs = (
        P(("groups", "dp"), "rep", None, None),
        P("groups", "rep"),
        P("groups", "rep"),
        P("groups", None),
        P(("groups", "dp"), None),
        P(("groups", "dp"), None),
        P("dp", None, None),
        P("dp", "rep"),
        P(("groups", "dp"), "rep"),
        P("rep"),
        P("rep", "dp"),
        P("rep", "dp"),
        P("dp", "rep"),
    )
    out_specs = P(("groups", "dp"), "rep")
    return jax.shard_map(
        on_device, mesh=mesh, in_specs=in_specs, out_specs=out_specs, check_vma=False
    )
```

profile of v0, /device:TPU:0, one launch (start us, length us, event | category | flops | bytes accessed | tf_op | source)
XLA Modules:
  0.0 225.6 jit_solution(1305932446610789168)
XLA Ops:
  9.0 3.5 %gather_fusion = bf16[12,576,128]{2,1,0:T(8,128)(2,1)} fusion(bf16[12,576,128]{2,1,0:T(8,128)(2,1)} %bitcast.145, s32[1024]{0:T(1024)S(1)} %pad_clamp_fusion.1), kind=kCustom, calls=%fused_computation.clone | custom fusion | bytes 3538992 | tf_op jit(solution)/shard_map/jit(_take)/gather | solution.py:145
  12.5 2.9 %select_select_fusion = bf16[12,576,128]{2,1,0:T(8,128)(2,1)} fusion(bf16[12,576,128]{2,1,0:T(8,128)(2,1)} %gather_fusion, pred[12]{0:T(512)(128)(4,1)S(1)} %get-tuple-element.237, pred[12]{0:T(512)(128)(4,1)S(1)} %broadcast_in_dim.122), kind=kLoop, calls=%fused_computation.26 | loop fusion | flops 1769472 | bytes 3538968 | tf_op jit(solution)/shard_map/jit(_where)/select_n | solution.py:146
  15.4 6.5 %all-to-all-start = ((bf16[12,576,128]{2,1,0:T(8,128)(2,1)}), bf16[12,576,128]{2,1,0:T(8,128)(2,1)}, u32[]{:S(2)}, u32[]{:S(2)}) async-start(bf16[12,576,128]{2,1,0:T(8,128)(2,1)} %select_select_fusion), calls=%async_computation | async-start | bytes 3538944 | tf_op jit(solution)/shard_map/all_to_all | solution.py:147
  23.8 39.4 %all-to-all-done = bf16[12,576,128]{2,1,0:T(8,128)(2,1)} async-done(((bf16[12,576,128]{2,1,0:T(8,128)(2,1)}), bf16[12,576,128]{2,1,0:T(8,128)(2,1)}, u32[]{:S(2)}, u32[]{:S(2)}) %all-to-all-start) | async-done | bytes 1769504 | tf_op jit(solution)/shard_map/all_to_all | solution.py:147
  63.2 3.5 %gather_fusion.1 = bf16[12,576,128]{2,1,0:T(8,128)(2,1)} fusion(bf16[12,576,128]{2,1,0:T(8,128)(2,1)} %all-to-all-done, s32[1024]{0:T(1024)S(1)} %pad_clamp_fusion), kind=kCustom, calls=%fused_computation.1.clone | custom fusion | bytes 3538992 | tf_op jit(solution)/shard_map/jit(_take)/gather | solution.py:148
  66.7 1.7 broadcast_select_fusion
  69.8 2.3 %fusion.13 = f32[12,2,64,512]{3,2,1,0:T(8,128)} fusion(bf16[12,576,128]{2,1,0:T(8,128)(2,1)S(1)} %broadcast_select_fusion, f32[12,2,64,128]{3,2,1,0:T(8,128)S(1)} %get-tuple-element.233, f32[12,2,64]{2,1,0:T(2,128)S(1)} %get-tuple-element.232, s32[12]{0:T(128)S(1)} %fusion.60), kind=kOutput, calls=%fused_computation.29 | convolution fusion | flops 202113024 | bytes 5517824 | tf_op jit(solution)/shard_map/psht,pct->pshc/dot_general | solution.py:46
  72.4 5.1 %all_gather.20 = bf16[4,1,2,64]{3,2,1,0:T(2,128)(2,1)S(1)} all-gather(bf16[1,1,2,64]{3,2,1,0:T(2,128)(2,1)S(1)} %fusion.50), channel_id=1, replica_groups=mesh['groups'=2,'dp'=4,'rep'=4] {'rep'}, dimensions={0}, use_global_device_ids=true | all-gather | bytes 1280 | tf_op jit(solution)/shard_map/all_gather | solution.py:18
  77.5 7.4 %fusion.7 = f32[2,64,1,512]{3,2,1,0:T(1,128)S(1)} fusion(f32[12,2,64,1]{0,3,2,1:T(1,128)S(1)} %copy.29, f32[12,2,64,512]{3,2,1,0:T(8,128)} %fusion.13), kind=kOutput, calls=%fused_computation.16 | convolution fusion | flops 9437184 | bytes 3414016 | tf_op jit(solution)/shard_map/jpsh,pshc->jshc/dot_general | solution.py:60
  85.2 7.3 %all-gather = bf16[8,64,512]{2,1,0:T(8,128)(2,1)S(1)} all-gather(bf16[2,64,512]{2,1,0:T(8,128)(2,1)S(1)} %fusion.25), channel_id=2, replica_groups=mesh['groups'=2,'dp'=4,'rep'=4] {'rep'}, dimensions={0}, use_global_device_ids=true | all-gather | bytes 655360 | tf_op jit(solution)/shard_map/all_gather | solution.py:18
  92.5 5.1 %all_gather.19 = bf16[4,1,2,64]{3,2,1,0:T(2,128)(2,1)S(1)} all-gather(bf16[1,1,2,64]{3,2,1,0:T(2,128)(2,1)S(1)} %fusion.54), channel_id=1, replica_groups=mesh['groups'=2,'dp'=4,'rep'=4] {'rep'}, dimensions={0}, use_global_device_ids=true | all-gather | bytes 1280 | tf_op jit(solution)/shard_map/all_gather | solution.py:18
  98.2 1.0 fusion.38
  99.2 3.3 %all-to-all-start.1 = ((bf16[2,64,512]{2,0,1:T(2,128)(2,1)}), bf16[2,64,512]{2,0,1:T(2,128)(2,1)S(1)}, u32[]{:S(2)}, u32[]{:S(2)}) async-start(bf16[2,64,512]{2,0,1:T(2,128)(2,1)} %fusion.38), calls=%async_computation.1 | async-start | bytes 262144 | tf_op jit(solution)/shard_map/all_to_all | solution.py:157
  103.8 5.2 %all-to-all-done.1 = bf16[2,64,512]{2,0,1:T(2,128)(2,1)S(1)} async-done(((bf16[2,64,512]{2,0,1:T(2,128)(2,1)}), bf16[2,64,512]{2,0,1:T(2,128)(2,1)S(1)}, u32[]{:S(2)}, u32[]{:S(2)}) %all-to-all-start.1) | async-done | bytes 131104 | tf_op jit(solution)/shard_map/all_to_all | solution.py:157
  109.2 4.4 %convolution_convert_fusion.3 = bf16[8,1792]{1,0:T(8,128)(2,1)S(1)} fusion(bf16[2048,1792]{1,0:T(8,128)(2,1)} %param.24, bf16[8,16,512]{2,0,1:T(8,128)(2,1)S(1)} %all_to_all.20, bf16[16,512,128]{2,1,0:T(8,128)(2,1)S(1)} %copy-done), kind=kOutput, calls=%fused_computation.21 | convolution fusion | flops 75528192 | bytes 9596928 | tf_op jit(solution)/shard_map/dot_general | solution.py:162
  113.6 17.5 %all-reduce = bf16[8,1792]{1,0:T(8,128)(2,1)S(1)} all-reduce(bf16[8,1792]{1,0:T(8,128)(2,1)S(1)} %convolution_convert_fusion.3), channel_id=3, replica_groups=mesh['groups'=2,'dp'=4,'rep'=4] {'dp'}, use_global_device_ids=true, to_apply=%region_12.14.clone | all-reduce | flops 14336 | bytes 57344
  131.2 5.8 %psum.14 = f32[2]{0:T(128)S(1)} all-reduce(f32[2]{0:T(128)S(1)} %multiply_reduce_fusion), channel_id=1, replica_groups=mesh['groups'=2,'dp'=4,'rep'=4] {'rep'}, use_global_device_ids=true, to_apply=%region_14.16 | all-reduce | flops 2 | bytes 16 | tf_op jit(solution)/shard_map/psum | solution.py:168
  137.1 13.2 %all-gather.1 = bf16[4,2,1792]{2,1,0:T(2,128)(2,1)S(1)} all-gather(bf16[1,2,1792]{2,1,0:T(2,128)(2,1)S(1)} %fusion.43), channel_id=1, replica_groups=mesh['groups'=2,'dp'=4,'rep'=4] {'dp'}, dimensions={0}, use_global_device_ids=true | all-gather | bytes 35840 | tf_op jit(solution)/shard_map/all_gather | solution.py:172
  150.3 5.7 %convolution_convert_fusion = bf16[8,3072]{1,0:T(8,128)(2,1)S(1)} fusion(bf16[8,1792]{1,0:T(8,128)(2,1)S(1)} %reshape.433, bf16[1792,3072]{1,0:T(8,128)(2,1)} %param.28), kind=kOutput, calls=%fused_computation.18 | convolution fusion | flops 88104960 | bytes 11087872 | tf_op jit(solution)/shard_map/dot_general | solution.py:174
  156.0 5.7 %convolution_convert_fusion.1 = bf16[8,3072]{1,0:T(8,128)(2,1)S(1)} fusion(bf16[8,1792]{1,0:T(8,128)(2,1)S(1)} %reshape.433, bf16[1792,3072]{1,0:T(8,128)(2,1)} %param.27), kind=kOutput, calls=%fused_computation.19 | convolution fusion | flops 88104960 | bytes 11087872 | tf_op jit(solution)/shard_map/dot_general | solution.py:173
  162.3 30.3 %all-reduce.4.cloned.1.call-done = bf16[8,6144]{1,0:T(8,128)(2,1)} async-done(((bf16[8,6144]{1,0:T(8,128)(2,1)}), bf16[8,6144]{1,0:T(8,128)(2,1)}) %all-reduce.4.cloned.1.call-update) | async-done | bytes 98320 | tf_op jit(solution)/shard_map/psum | solution.py:176
  192.6 0.9 convert_element_type.203
  193.5 5.7 %convolution_convert_fusion.2 = bf16[8,1792]{1,0:T(8,128)(2,1)S(1)} fusion(bf16[3072,1792]{1,0:T(8,128)(2,1)} %param.29, f32[8,6144]{1,0:T(8,128)S(1)} %convert_element_type.203), kind=kOutput, calls=%fused_computation.20 | convolution fusion | flops 88242176 | bytes 11235328 | tf_op jit(solution)/shard_map/dot_general | solution.py:183
  199.2 19.0 %all-reduce.1 = bf16[8,1792]{1,0:T(8,128)(2,1)S(1)} all-reduce(bf16[8,1792]{1,0:T(8,128)(2,1)S(1)} %convolution_convert_fusion.2), channel_id=4, replica_groups=mesh['groups'=2,'dp'=4,'rep'=4] {'dp'}, use_global_device_ids=true, to_apply=%region_16.18.clone | all-reduce | flops 14336 | bytes 57344
  (74 shorter events, 9.7 us)
Async XLA Ops:
  6.5 102.6 %copy-start = (bf16[16,512,128]{2,1,0:T(8,128)(2,1)S(1)}, bf16[16,512,128]{2,1,0:T(8,128)(2,1)}, u32[]{:S(2)}) copy-start(bf16[16,512,128]{2,1,0:T(8,128)(2,1)} %param.23) | copy-start | bytes 6291460
  15.4 6.5 %copy-start.1 = (bf16[2,36864]{1,0:T(2,128)(2,1)S(1)}, bf16[2,36864]{1,0:T(2,128)(2,1)}, u32[]{:S(2)}) copy-start(bf16[2,36864]{1,0:T(2,128)(2,1)} %param.21) | copy-start | bytes 442372
  15.4 6.7 %copy-start.6 = (s32[4,1]{0,1:T(1,128)S(1)}, s32[4,1]{0,1:T(1,128)}, u32[]{:S(2)}) copy-start(s32[4,1]{0,1:T(1,128)} %param.20) | copy-start | bytes 52
  15.4 7.3 %copy-start.5 = (s32[4,12]{1,0:T(4,128)S(1)}, s32[4,12]{1,0:T(4,128)}, u32[]{:S(2)}) copy-start(s32[4,12]{1,0:T(4,128)} %param.18) | copy-start | bytes 580
  15.4 8.1 %copy-start.3 = (bf16[2,576]{1,0:T(2,128)(2,1)S(1)}, bf16[2,576]{1,0:T(2,128)(2,1)}, u32[]{:S(2)}) copy-start(bf16[2,576]{1,0:T(2,128)(2,1)} %param.22) | copy-start | bytes 6916
  15.4 47.8 %all-to-all-start = ((bf16[12,576,128]{2,1,0:T(8,128)(2,1)}), bf16[12,576,128]{2,1,0:T(8,128)(2,1)}, u32[]{:S(2)}, u32[]{:S(2)}) async-start(bf16[12,576,128]{2,1,0:T(8,128)(2,1)} %select_select_fusion), calls=%async_computation | async-start | bytes 3538944 | tf_op jit(solution)/shard_map/all_to_all | solution.py:147
  97.5 5.0 %copy-start.7 = (u32[32]{0:T(128)S(1)}, u32[32]{0:T(128)}, u32[]{:S(2)}) copy-start(u32[32]{0:T(128)} %constant.150) | copy-start | bytes 388
  99.2 9.8 %all-to-all-start.1 = ((bf16[2,64,512]{2,0,1:T(2,128)(2,1)}), bf16[2,64,512]{2,0,1:T(2,128)(2,1)S(1)}, u32[]{:S(2)}, u32[]{:S(2)}) async-start(bf16[2,64,512]{2,0,1:T(2,128)(2,1)} %fusion.38), calls=%async_computation.1 | async-start | bytes 262144 | tf_op jit(solution)/shard_map/all_to_all | solution.py:157
  102.5 90.1 %all-reduce.4.cloned.1.call-start = ((), (), s32[]{:S(2)}) async-start(), calls=%async_computation.2 | async-start | bytes 196608 | tf_op jit(solution)/shard_map/psum | solution.py:176
  109.2 21.9 %copy-start.2 = (bf16[2,1792]{1,0:T(2,128)(2,1)S(1)}, bf16[2,1792]{1,0:T(2,128)(2,1)}, u32[]{:S(2)}) copy-start(bf16[2,1792]{1,0:T(2,128)(2,1)} %param.25) | copy-start | bytes 21508
  109.2 27.9 %copy-start.4 = (f32[1792]{0:T(1024)S(1)}, f32[1792]{0:T(1024)}, u32[]{:S(2)}) copy-start(f32[1792]{0:T(1024)} %param.26) | copy-start | bytes 21508
Sparse Core Ops, SparseCore 0:
  162.4 30.1 all-reduce.3
where the time goes:
time: 226 us
  waiting for transfers between devices  74.9 us (33%)
  blocking collectives  72.8 us (32%)
  matrix products  32.4 us (14%)
  between operations  14.3 us (6%)
  other arithmetic  12.1 us (5%)
  starting transfers between devices  9.85 us (4%)
  local copies, waits for them, and re-layouts  9.15 us (4%)
    all_to_all x1, waiting for transfers between devices, on_device(): lax.all_to_all(outgoing, 'dp', split_axis=0, concat_axis=0, tiled=True)  39.4 us
    unnamed x2, blocking collectives  36.4 us
    psum x1, waiting for transfers between devices, on_device(): lax.psum(partial_rows.astype(jnp.bfloat16), 'rep').astype(jnp.float32)  30.3 us
    all_gather x3, blocking collectives, merged_2(): lax.all_gather(a.astype(kind), axis)  17.4 us
    all_gather x1, blocking collectives, on_device(): piece = lax.all_gather(normed, 'dp', axis=0, tiled=True)  13.2 us
    dot_general x1, matrix products, join_pages(): jnp.einsum('jpsh,pshc->jshc', factor, partial_value, precision=lax.Precis...  7.4 us
    all_to_all x1, starting transfers between devices, on_device(): lax.all_to_all(outgoing, 'dp', split_axis=0, concat_axis=0, tiled=True)  6.49 us
    psum x1, blocking collectives, on_device(): squares = lax.psum(jnp.sum(mixed_rows * mixed_rows, axis=1), 'rep')  5.84 us
  transfers between devices with their start and end apart: 3, of which 3 were waited for; matrix products, arithmetic and copies ran while one was open for 1% of the time, Pallas kernels for 0%

commit v1 on v0

--- a/solution.py
+++ b/solution.py
@@ -173,7 +173,9 @@
     gate_part = jnp.dot(piece, w_gate, preferred_element_type=jnp.float32)
     up_part = jnp.dot(piece, w_up, preferred_element_type=jnp.float32)
     partial_rows = jnp.concatenate([gate_part, up_part], axis=1)
-    gate_up = lax.psum(partial_rows.astype(jnp.bfloat16), "rep").astype(jnp.float32)
+    gate_up = jnp.sum(
+        jax.lax.all_gather(partial_rows.astype(jnp.bfloat16), axis_name="rep"), 0
+    ).astype(jnp.float32)
     hidden_width = w_gate.shape[1]
     hidden = (jax.nn.silu(gate_up[:, :hidden_width]) * gate_up[:, hidden_width:]).astype(
         jnp.bfloat16

time: 226 us -> 185 us (0.82)
  waiting for transfers between devices: 74.9 us -> 44.6 us
  between operations: 14.3 us -> 0.89 us
  blocking collectives: 72.8 us -> 76.4 us
    psum x1 -> x0, waiting for transfers between devices: 30.3 us -> none  [on_device(): lax.psum(partial_rows.astype(jnp.bfloat16), 'rep').astype(jnp.float32)]
    all_gather x0 -> x1, blocking collectives: none -> 6.68 us  [on_device(): jax.lax.all_gather(partial_rows.astype(jnp.bfloat16), axis_name='rep')]
    unnamed x2, blocking collectives: 36.4 us -> 33.3 us
  transfers between devices with their start and end apart: 3 -> 2, of which waited for: 3 -> 2; matrix products, arithmetic and copies ran while one was open for 1% -> 1% of each run, Pallas kernels for 0% -> 0%
where the time goes in v1:
time: 185 us; the launch traced here: 184 us
  blocking collectives  76.4 us (41%)
  waiting for transfers between devices  44.6 us (24%)
  matrix products  32.4 us (18%)
  other arithmetic  10.7 us (6%)
  starting transfers between devices  9.81 us (5%)
  local copies, waits for them, and re-layouts  9.15 us (5%)
    all_to_all x1, waiting for transfers between devices, on_device(): lax.all_to_all(outgoing, 'dp', split_axis=0, concat_axis=0, tiled=True)  39.4 us
    unnamed x2, blocking collectives  33.3 us
    all_gather x3, blocking collectives, merged_2(): lax.all_gather(a.astype(kind), axis)  17.4 us
    all_gather x1, blocking collectives, on_device(): piece = lax.all_gather(normed, 'dp', axis=0, tiled=True)  13.4 us
    dot_general x1, matrix products, join_pages(): jnp.einsum('jpsh,pshc->jshc', factor, partial_value, precision=lax.Precis...  7.4 us
    all_gather x1, blocking collectives, on_device(): jax.lax.all_gather(partial_rows.astype(jnp.bfloat16), axis_name='rep')  6.68 us
    all_to_all x1, starting transfers between devices, on_device(): lax.all_to_all(outgoing, 'dp', split_axis=0, concat_axis=0, tiled=True)  6.49 us
    dot_general x1, matrix products, on_device(): gate_part = jnp.dot(piece, w_gate, preferred_element_type=jnp.float32)  5.66 us
  transfers between devices with their start and end apart: 2, of which 2 were waited for; matrix products, arithmetic and copies ran while one was open for 1% of the time, Pallas kernels for 0%

profile of v1, /device:TPU:0, one launch (start us, length us, event | category | flops | bytes accessed | tf_op | source)
XLA Modules:
  0.0 184.1 jit_solution(6700640061107649459)
XLA Ops:
  0.0 0.8 fusion.68
  2.4 3.5 %gather_fusion = bf16[12,576,128]{2,1,0:T(8,128)(2,1)} fusion(bf16[12,576,128]{2,1,0:T(8,128)(2,1)} %bitcast.149, s32[1024]{0:T(1024)S(1)} %pad_clamp_fusion.1), kind=kCustom, calls=%fused_computation.clone | custom fusion | bytes 3538992 | tf_op jit(solution)/shard_map/jit(_take)/gather | solution.py:145
  5.9 2.9 %select_select_fusion = bf16[12,576,128]{2,1,0:T(8,128)(2,1)} fusion(bf16[12,576,128]{2,1,0:T(8,128)(2,1)} %gather_fusion, pred[12]{0:T(512)(128)(4,1)S(1)} %get-tuple-element.237, pred[12]{0:T(512)(128)(4,1)S(1)} %broadcast_in_dim.122), kind=kLoop, calls=%fused_computation.28 | loop fusion | flops 1769472 | bytes 3538968 | tf_op jit(solution)/shard_map/jit(_where)/select_n | solution.py:146
  8.9 6.5 %all-to-all-start = ((bf16[12,576,128]{2,1,0:T(8,128)(2,1)}), bf16[12,576,128]{2,1,0:T(8,128)(2,1)}, u32[]{:S(2)}, u32[]{:S(2)}) async-start(bf16[12,576,128]{2,1,0:T(8,128)(2,1)} %select_select_fusion), calls=%async_computation | async-start | bytes 3538944 | tf_op jit(solution)/shard_map/all_to_all | solution.py:147
  17.3 39.4 %all-to-all-done = bf16[12,576,128]{2,1,0:T(8,128)(2,1)} async-done(((bf16[12,576,128]{2,1,0:T(8,128)(2,1)}), bf16[12,576,128]{2,1,0:T(8,128)(2,1)}, u32[]{:S(2)}, u32[]{:S(2)}) %all-to-all-start) | async-done | bytes 1769504 | tf_op jit(solution)/shard_map/all_to_all | solution.py:147
  56.7 3.5 %gather_fusion.1 = bf16[12,576,128]{2,1,0:T(8,128)(2,1)} fusion(bf16[12,576,128]{2,1,0:T(8,128)(2,1)} %all-to-all-done, s32[1024]{0:T(1024)S(1)} %pad_clamp_fusion), kind=kCustom, calls=%fused_computation.1.clone | custom fusion | bytes 3538992 | tf_op jit(solution)/shard_map/jit(_take)/gather | solution.py:148
  60.2 1.7 broadcast_select_fusion
  63.3 2.3 %fusion.15 = f32[12,2,64,512]{3,2,1,0:T(8,128)} fusion(bf16[12,576,128]{2,1,0:T(8,128)(2,1)S(1)} %broadcast_select_fusion, f32[12,2,64,128]{3,2,1,0:T(8,128)S(1)} %get-tuple-element.233, f32[12,2,64]{2,1,0:T(2,128)S(1)} %get-tuple-element.232, s32[12]{0:T(128)S(1)} %fusion.62), kind=kOutput, calls=%fused_computation.31 | convolution fusion | flops 202113024 | bytes 5517824 | tf_op jit(solution)/shard_map/psht,pct->pshc/dot_general | solution.py:46
  65.8 5.1 %all_gather.24 = bf16[4,1,2,64]{3,2,1,0:T(2,128)(2,1)S(1)} all-gather(bf16[1,1,2,64]{3,2,1,0:T(2,128)(2,1)S(1)} %fusion.52), channel_id=1, replica_groups=mesh['groups'=2,'dp'=4,'rep'=4] {'rep'}, dimensions={0}, use_global_device_ids=true | all-gather | bytes 1280 | tf_op jit(solution)/shard_map/all_gather | solution.py:18
  71.0 7.4 %fusion.7 = f32[2,64,1,512]{3,2,1,0:T(1,128)S(1)} fusion(f32[12,2,64,1]{0,3,2,1:T(1,128)S(1)} %copy.29, f32[12,2,64,512]{3,2,1,0:T(8,128)} %fusion.15), kind=kOutput, calls=%fused_computation.16 | convolution fusion | flops 9437184 | bytes 3414016 | tf_op jit(solution)/shard_map/jpsh,pshc->jshc/dot_general | solution.py:60
  78.6 7.3 %all-gather = bf16[8,64,512]{2,1,0:T(8,128)(2,1)S(1)} all-gather(bf16[2,64,512]{2,1,0:T(8,128)(2,1)S(1)} %fusion.27), channel_id=2, replica_groups=mesh['groups'=2,'dp'=4,'rep'=4] {'rep'}, dimensions={0}, use_global_device_ids=true | all-gather | bytes 655360 | tf_op jit(solution)/shard_map/all_gather | solution.py:18
  85.9 5.1 %all_gather.23 = bf16[4,1,2,64]{3,2,1,0:T(2,128)(2,1)S(1)} all-gather(bf16[1,1,2,64]{3,2,1,0:T(2,128)(2,1)S(1)} %fusion.56), channel_id=1, replica_groups=mesh['groups'=2,'dp'=4,'rep'=4] {'rep'}, dimensions={0}, use_global_device_ids=true | all-gather | bytes 1280 | tf_op jit(solution)/shard_map/all_gather | solution.py:18
  91.7 1.0 fusion.40
  92.7 3.3 %all-to-all-start.1 = ((bf16[2,64,512]{2,0,1:T(2,128)(2,1)}), bf16[2,64,512]{2,0,1:T(2,128)(2,1)S(1)}, u32[]{:S(2)}, u32[]{:S(2)}) async-start(bf16[2,64,512]{2,0,1:T(2,128)(2,1)} %fusion.40), calls=%async_computation.1 | async-start | bytes 262144 | tf_op jit(solution)/shard_map/all_to_all | solution.py:157
  97.2 5.2 %all-to-all-done.1 = bf16[2,64,512]{2,0,1:T(2,128)(2,1)S(1)} async-done(((bf16[2,64,512]{2,0,1:T(2,128)(2,1)}), bf16[2,64,512]{2,0,1:T(2,128)(2,1)S(1)}, u32[]{:S(2)}, u32[]{:S(2)}) %all-to-all-start.1) | async-done | bytes 131104 | tf_op jit(solution)/shard_map/all_to_all | solution.py:157
  102.6 4.4 %convolution_convert_fusion.3 = bf16[8,1792]{1,0:T(8,128)(2,1)S(1)} fusion(bf16[2048,1792]{1,0:T(8,128)(2,1)} %param.24, bf16[8,16,512]{2,0,1:T(8,128)(2,1)S(1)} %all_to_all.20, bf16[16,512,128]{2,1,0:T(8,128)(2,1)S(1)} %copy-done), kind=kOutput, calls=%fused_computation.23 | convolution fusion | flops 75528192 | bytes 9596928 | tf_op jit(solution)/shard_map/dot_general | solution.py:162
  107.1 17.5 %all-reduce = bf16[8,1792]{1,0:T(8,128)(2,1)S(1)} all-reduce(bf16[8,1792]{1,0:T(8,128)(2,1)S(1)} %convolution_convert_fusion.3), channel_id=3, replica_groups=mesh['groups'=2,'dp'=4,'rep'=4] {'dp'}, use_global_device_ids=true, to_apply=%region_12.14.clone | all-reduce | flops 14336 | bytes 57344
  124.7 5.7 %psum.7 = f32[2]{0:T(128)S(1)} all-reduce(f32[2]{0:T(128)S(1)} %multiply_reduce_fusion), channel_id=1, replica_groups=mesh['groups'=2,'dp'=4,'rep'=4] {'rep'}, use_global_device_ids=true, to_apply=%region_14.16 | all-reduce | flops 2 | bytes 16 | tf_op jit(solution)/shard_map/psum | solution.py:168
  130.4 13.4 %all-gather.1 = bf16[4,2,1792]{2,1,0:T(2,128)(2,1)S(1)} all-gather(bf16[1,2,1792]{2,1,0:T(2,128)(2,1)S(1)} %fusion.45), channel_id=1, replica_groups=mesh['groups'=2,'dp'=4,'rep'=4] {'dp'}, dimensions={0}, use_global_device_ids=true | all-gather | bytes 35840 | tf_op jit(solution)/shard_map/all_gather | solution.py:172
  143.8 5.7 %fusion.10 = bf16[1,8,3072]{2,1,0:T(8,128)(2,1)S(1)} fusion(bf16[8,1792]{1,0:T(8,128)(2,1)S(1)} %reshape.464, bf16[1792,3072]{1,0:T(8,128)(2,1)} %param.28), kind=kOutput, calls=%fused_computation.21 | convolution fusion | flops 88104960 | bytes 11087872 | tf_op jit(solution)/shard_map/dot_general | solution.py:174
  149.5 5.7 %fusion.9 = bf16[1,8,3072]{2,1,0:T(8,128)(2,1)S(1)} fusion(bf16[8,1792]{1,0:T(8,128)(2,1)S(1)} %reshape.464, bf16[1792,3072]{1,0:T(8,128)(2,1)} %param.27), kind=kOutput, calls=%fused_computation.20 | convolution fusion | flops 88104960 | bytes 11087872 | tf_op jit(solution)/shard_map/dot_general | solution.py:173
  155.1 6.7 %all_gather.26 = bf16[4,8,6144]{2,1,0:T(8,128)(2,1)S(1)} all-gather(bf16[1,8,6144]{2,1,0:T(8,128)(2,1)S(1)} %pad_maximum_fusion), channel_id=1, replica_groups=mesh['groups'=2,'dp'=4,'rep'=4] {'rep'}, dimensions={0}, use_global_device_ids=true | all-gather | bytes 491520 | tf_op jit(solution)/shard_map/all_gather | solution.py:177
  161.9 5.7 %convolution_convert_fusion.2 = bf16[8,1792]{1,0:T(8,128)(2,1)S(1)} fusion(bf16[3072,1792]{1,0:T(8,128)(2,1)} %param.29, f32[8,6144]{1,0:T(8,128)S(1)} %convert_element_type.212), kind=kOutput, calls=%fused_computation.22 | convolution fusion | flops 88242176 | bytes 11235328 | tf_op jit(solution)/shard_map/dot_general | solution.py:185
  167.6 15.9 %all-reduce.1 = bf16[8,1792]{1,0:T(8,128)(2,1)S(1)} all-reduce(bf16[8,1792]{1,0:T(8,128)(2,1)S(1)} %convolution_convert_fusion.2), channel_id=4, replica_groups=mesh['groups'=2,'dp'=4,'rep'=4] {'dp'}, use_global_device_ids=true, to_apply=%region_16.18.clone | all-reduce | flops 14336 | bytes 57344
  (73 shorter events, 8.2 us)
Async XLA Ops:
  0.0 102.6 %copy-start = (bf16[16,512,128]{2,1,0:T(8,128)(2,1)S(1)}, bf16[16,512,128]{2,1,0:T(8,128)(2,1)}, u32[]{:S(2)}) copy-start(bf16[16,512,128]{2,1,0:T(8,128)(2,1)} %param.23) | copy-start | bytes 6291460
  8.9 6.5 %copy-start.1 = (bf16[2,36864]{1,0:T(2,128)(2,1)S(1)}, bf16[2,36864]{1,0:T(2,128)(2,1)}, u32[]{:S(2)}) copy-start(bf16[2,36864]{1,0:T(2,128)(2,1)} %param.21) | copy-start | bytes 442372
  8.9 6.7 %copy-start.6 = (s32[4,1]{0,1:T(1,128)S(1)}, s32[4,1]{0,1:T(1,128)}, u32[]{:S(2)}) copy-start(s32[4,1]{0,1:T(1,128)} %param.20) | copy-start | bytes 52
  8.9 7.3 %copy-start.5 = (s32[4,12]{1,0:T(4,128)S(1)}, s32[4,12]{1,0:T(4,128)}, u32[]{:S(2)}) copy-start(s32[4,12]{1,0:T(4,128)} %param.18) | copy-start | bytes 580
  8.9 8.1 %copy-start.3 = (bf16[2,576]{1,0:T(2,128)(2,1)S(1)}, bf16[2,576]{1,0:T(2,128)(2,1)}, u32[]{:S(2)}) copy-start(bf16[2,576]{1,0:T(2,128)(2,1)} %param.22) | copy-start | bytes 6916
  8.9 47.8 %all-to-all-start = ((bf16[12,576,128]{2,1,0:T(8,128)(2,1)}), bf16[12,576,128]{2,1,0:T(8,128)(2,1)}, u32[]{:S(2)}, u32[]{:S(2)}) async-start(bf16[12,576,128]{2,1,0:T(8,128)(2,1)} %select_select_fusion), calls=%async_computation | async-start | bytes 3538944 | tf_op jit(solution)/shard_map/all_to_all | solution.py:147
  91.0 5.0 %copy-start.7 = (u32[32]{0:T(128)S(1)}, u32[32]{0:T(128)}, u32[]{:S(2)}) copy-start(u32[32]{0:T(128)} %constant.151) | copy-start | bytes 388
  92.7 9.8 %all-to-all-start.1 = ((bf16[2,64,512]{2,0,1:T(2,128)(2,1)}), bf16[2,64,512]{2,0,1:T(2,128)(2,1)S(1)}, u32[]{:S(2)}, u32[]{:S(2)}) async-start(bf16[2,64,512]{2,0,1:T(2,128)(2,1)} %fusion.40), calls=%async_computation.1 | async-start | bytes 262144 | tf_op jit(solution)/shard_map/all_to_all | solution.py:157
  102.6 21.9 %copy-start.2 = (bf16[2,1792]{1,0:T(2,128)(2,1)S(1)}, bf16[2,1792]{1,0:T(2,128)(2,1)}, u32[]{:S(2)}) copy-start(bf16[2,1792]{1,0:T(2,128)(2,1)} %param.25) | copy-start | bytes 21508
  102.6 27.7 %copy-start.4 = (f32[1792]{0:T(1024)S(1)}, f32[1792]{0:T(1024)}, u32[]{:S(2)}) copy-start(f32[1792]{0:T(1024)} %param.26) | copy-start | bytes 21508
